TPU v7x, 32 devices: a whole 2x2x4 slice. The times are simulated.
32 devices in a mesh: req: 8 (over z, x), cfg: 2 (over core), seq: 2 (over y).
Axes of the slice: x: 2, y: 2, z: 4, core: 2. Of those that a mesh axis runs over, the one named last changes fastest.
Arguments:
- queries: bfloat16 [8, 2, 512, 1024], P('req', 'cfg', 'seq'), may hold values from -48 to 48
- key_vectors: bfloat16 [8, 2, 512, 1024], P('req', 'cfg', 'seq'), may hold values from -48 to 48
- values: bfloat16 [8, 2, 512, 1024], P('req', 'cfg', 'seq'), may hold values from -6 to 6
- hidden: bfloat16 [8, 2, 512, 1536], P('req', 'cfg', 'seq'), may hold values from -15 to 15
- out_proj: bfloat16 [1024, 1536], P('req'), may hold values from -0.1875 to 0.1875
- head_weight: bfloat16 [1536, 64], replicated, may hold values from -0.15625 to 0.15625
- head_bias: float32 [64], replicated, may hold values from -3 to 3
- attn_gate: float32 [8, 1536], P('req'), may hold values from 0.5 to 4
- shift_scale: float32 [8, 2, 1536], P('req'), may hold values from -3 to 3
- grid_shape: int32 [8, 3], P('req'), may hold values from 1 to 32, as said below
- step_index: int32 [8], P('req'), may hold values from 0 to 19
- guide_scale: float32 [8], P('req'), may hold values from 3 to 6
- latent: float32 [8, 512, 64], P('req', 'seq', 'cfg'), may hold values from -6 to 6
Outputs:
- next_latent: float32 [8, 512, 64], P('req', 'seq', 'cfg')
- velocity: float32 [8, 512, 64], P('req', 'seq', 'cfg')
Inputs may be any that keep to these rules, and one draw needn't show every extreme that they name: `grid_shape`: the frames are at most 2, the height at most 8 and the width at most 32, so that frames * height * width is at most 512; in every draw some request fills all 512 slots.
All inputs are finite; a program needn't handle non-finite values.
Results may differ from a plain program's by a relative error of at most 0.0052.
Values may be sent and summed in bfloat16 or wider, within the bound.
A program may use at most 64 MiB of HBM per device.

v0:
```python
import math
import jax
import jax.numpy as jnp
from jax import lax
from jax.sharding import PartitionSpec as P

HEAD_DIM = 128
STEPS = 20
masked_score = -1e30
norm_eps = 1e-06
shift_factor = 5.0


def partner_2(block, axis, distance):
    count = lax.axis_size(axis)
    route = []
    for low in range(count):
        high = low | 1 << distance
        if high != low and high < count:
            route += [(low, high), (high, low)]
    return lax.ppermute(block, axis, route)


def rotary(vectors, grid_dims, first_token):
    row_count, col_count = vectors.shape
    sixth_dim = HEAD_DIM // 6
    time_pairs = (HEAD_DIM - 4 * sixth_dim) // 2
    column = jnp.arange(col_count, dtype=jnp.int32) % HEAD_DIM
    pair_index = column // 2
    space_pair = (pair_index - time_pairs).astype(jnp.float32)
    is_time = pair_index < time_pairs
    is_height = jnp.logical_and(pair_index >= time_pairs, pair_index < time_pairs + sixth_dim)
    exponent = jnp.where(
        is_time,
        pair_index.astype(jnp.float32) / time_pairs,
        jnp.where(is_height, space_pair / sixth_dim, (space_pair - sixth_dim) / sixth_dim),
    )
    frequency = jnp.power(jnp.float32(10000.0), -exponent)
    token_ids = first_token + jnp.arange(row_count, dtype=jnp.int32)
    plane_size = grid_dims[1] * grid_dims[2]
    frame_ids = token_ids // plane_size
    height = token_ids // grid_dims[2] % grid_dims[1]
    across = token_ids % grid_dims[2]
    position = jnp.where(
        is_time[None, :],
        frame_ids[:, None],
        jnp.where(is_height[None, :], height[:, None], across[:, None]),
    ).astype(jnp.float32)
    angles = position * frequency[None, :]
    is_even = column % 2 == 0
    source = vectors.astype(jnp.float32)
    partner = jnp.where(is_even[None, :], jnp.roll(source, -1, axis=1), jnp.roll(source, 1, axis=1))
    sign_flip = jnp.where(is_even, -1.0, 1.0).astype(jnp.float32)
    turned = source * jnp.cos(angles) + partner * (jnp.sin(angles) * sign_flip[None, :])
    return turned.astype(jnp.bfloat16)


def noise_level(step_value):
    progress = 1.0 - step_value.astype(jnp.float32) / STEPS
    return shift_factor * progress / (1.0 + (shift_factor - 1.0) * progress)


def output_head(hidden_rows, proj, gate_row, modulation, head_weight, head_bias):
    mixed_rows = hidden_rows.astype(jnp.float32) + gate_row[None, :] * proj
    average = jnp.mean(mixed_rows, axis=-1, keepdims=True)
    centered = mixed_rows - average
    spread = jnp.mean(centered * centered, axis=-1, keepdims=True)
    normed = centered * lax.rsqrt(spread + norm_eps)
    modded = (normed * (1.0 + modulation[1][None, :]) + modulation[0][None, :]).astype(jnp.bfloat16)
    return jnp.dot(modded, head_weight, preferred_element_type=jnp.float32) + head_bias[None, :]


def attend_all(query_heads, key_heads, value_heads, length):
    total_rows = query_heads.shape[0]
    block_rows = min(512, total_rows)
    score_scale = 1.0 / math.sqrt(HEAD_DIM)
    live_keys = jnp.arange(total_rows, dtype=jnp.int32) < length

    def one_block(start):
        query_block = lax.dynamic_slice_in_dim(query_heads, start, block_rows, 0)
        scores = (
            jnp.einsum("qhd,khd->hqk", query_block, key_heads, preferred_element_type=jnp.float32)
            * score_scale
        )
        scores = jnp.where(live_keys[None, None, :], scores, masked_score)
        row_max = jnp.max(scores, axis=-1, keepdims=True)
        exponent = jnp.exp(scores - row_max)
        row_sum = jnp.sum(exponent, axis=-1, keepdims=True)
        weights = (exponent / row_sum).astype(jnp.bfloat16)
        output = jnp.einsum(
            "hqk,khd->qhd", weights, value_heads, preferred_element_type=jnp.float32
        )
        return output.astype(jnp.bfloat16)

    starts = jnp.arange(total_rows // block_rows, dtype=jnp.int32) * block_rows
    return lax.map(one_block, starts).reshape(total_rows, -1)


def on_device(
    queries,
    key_vectors,
    values,
    hidden,
    out_proj,
    head_weight,
    head_bias,
    attn_gate,
    shift_scale,
    grid_shape,
    step_index,
    guide_scale,
    latent,
):
    row_count = queries.shape[2]
    grid_dims = grid_shape[0]
    length = grid_dims[0] * grid_dims[1] * grid_dims[2]
    first_token = lax.axis_index("seq") * row_count
    rot_q = rotary(queries[0, 0], grid_dims, first_token)
    rot_k = rotary(key_vectors[0, 0], grid_dims, first_token)
    head_q, head_k, head_v = (
        lax.all_to_all(rot_q, "seq", split_axis=1, concat_axis=0, tiled=True),
        lax.all_to_all(rot_k, "seq", split_axis=1, concat_axis=0, tiled=True),
        lax.all_to_all(values[0, 0], "seq", split_axis=1, concat_axis=0, tiled=True),
    )
    total_rows = head_q.shape[0]
    local_heads = head_q.shape[1] // HEAD_DIM
    head_shape = (total_rows, local_heads, HEAD_DIM)
    query_heads = head_q.reshape(head_shape)
    key_heads = head_k.reshape(head_shape)
    value_heads = head_v.reshape(head_shape)
    head_result = attend_all(query_heads, key_heads, value_heads, length)
    attended = lax.all_to_all(head_result, "seq", split_axis=0, concat_axis=1, tiled=True)
    proj = jnp.dot(
        attended,
        lax.all_gather(out_proj, "req", axis=0, tiled=True),
        preferred_element_type=jnp.float32,
    )
    prediction = output_head(
        hidden[0, 0], proj, attn_gate[0], shift_scale[0], head_weight, head_bias
    )
    own_width = latent.shape[2]
    cfg_place = lax.axis_index("cfg")
    own_cols = lax.dynamic_slice_in_dim(prediction, cfg_place * own_width, own_width, 1)
    partner_cols = lax.dynamic_slice_in_dim(prediction, (1 - cfg_place) * own_width, own_width, 1)
    other_half = partner_2(partner_cols, "cfg", 0)
    is_cond = cfg_place == 0
    cond_pred = jnp.where(is_cond, own_cols, other_half)
    uncond_pred = jnp.where(is_cond, other_half, own_cols)
    guided = uncond_pred + guide_scale[0] * (cond_pred - uncond_pred)
    live_rows = first_token + jnp.arange(row_count, dtype=jnp.int32) < length
    velocity = jnp.where(live_rows[:, None], guided, jnp.float32(0.0))
    delta_level = noise_level(step_index[0] + 1) - noise_level(step_index[0])
    next_latent = latent[0] + delta_level * velocity
    return (next_latent[None], velocity[None])


def solution(mesh):
    return jax.shard_map(
        on_device,
        mesh=mesh,
        in_specs=(
            P("req", "cfg", "seq", None),
            P("req", "cfg", "seq", None),
            P("req", "cfg", "seq", None),
            P("req", "cfg", "seq", None),
            P("req", None),
            P(),
            P(),
            P("req", None),
            P("req", None, None),
            P("req", None),
            P("req"),
            P("req"),
            P("req", "seq", "cfg"),
        ),
        out_specs=(P("req", "seq", "cfg"), P("req", "seq", "cfg")),
        check_vma=False,
    )
```

profile of v0, /device:TPU:1, one launch (start us, length us, event | category | flops | bytes accessed | tf_op | source)
XLA Modules:
  0.0 87.9 jit_solution(608926784474118634)
XLA Ops:
  7.2 0.7 all-gather.2.cloned.1.call-update
  7.9 1.4 %fusion.34 = (s32[1,1]{1,0:T(1,128)}, s32[1,1]{1,0:T(1,128)}, s32[1,1]{1,0:T(1,128)}) fusion(s32[1,3]{1,0:T(1,128)} %param.22), kind=kLoop, calls=%fused_computation.78 | loop fusion | bytes 24 | tf_op jit(solution)/shard_map/slice | solution.py:116
  14.0 2.1 %reshape.291 = f32[256,2,512]{2,1,0:T(2,128)S(1)} reshape(bf16[1,1,256,1024]{3,2,1,0:T(8,128)(2,1)} %param.13) | data formatting | bytes 1572864 | tf_op jit(solution)/shard_map/convert_element_type | solution.py:51
  16.1 2.1 %reshape.293 = f32[256,2,512]{2,1,0:T(2,128)S(1)} reshape(bf16[1,1,256,1024]{3,2,1,0:T(8,128)(2,1)} %param.14) | data formatting | bytes 1572864 | tf_op jit(solution)/shard_map/convert_element_type | solution.py:51
  18.3 0.9 %and_select_fusion.3 = (s32[256]{0:T(256)S(1)}, s32[256]{0:T(256)S(1)}) fusion(pred[]{:T(512)S(6)} %lt.119, s32[]{:T(128)S(6)} %select_n.201, s32[]{:T(128)S(6)} %mul.133, pred[]{:T(512)S(6)} %lt.117, s32[]{:T(128)S(6)} %select_n.199, s32[]{:T(128)} %bitcast.4, s32[]{:T(128)S(6)} %sign.48), kind=kLoop, calls=%fused_computation.61 | loop fusion | flops 5888 | bytes 2070 | tf_op jit(solution)/shard_map/jit(remainder)/select_n | solution.py:43
  19.5 0.4 fusion.32
  19.9 0.4 pad_maximum_fusion.2
  20.4 0.6 copy-done.2
  21.2 0.4 fusion.30
  21.6 0.4 pad_maximum_fusion
  22.1 5.4 %fusion.14 = (bf16[256,2,512]{2,0,1:T(8,128)(2,1)S(1)}, bf16[256,2,512]{2,0,1:T(8,128)(2,1)}) fusion(f32[32,2,8,512]{3,2,1,0:T(8,128)S(1)} %bitcast.64, f32[32,2,8,512]{3,2,1,0:T(8,128)S(1)} %bitcast.63, f32[256,2,512]{2,1,0:T(2,128)S(1)} %reshape.291, f32[2,512]{1,0:T(2,128)S(1)} %get-tuple-element.50, f32[2,512]{1,0:T(2,128)S(1)} %get-tuple-element.49, ...), kind=kLoop, calls=%fused_computation.23 | loop fusion | flops 3932160 | bytes 7354368 | tf_op jit(solution)/shard_map/convert_element_type | solution.py:55
  27.5 10.2 %all_to_all.61 = bf16[256,2,512]{2,0,1:T(8,128)(2,1)S(1)} all-to-all(bf16[256,2,512]{2,0,1:T(8,128)(2,1)S(1)} %get-tuple-element.32), channel_id=1, replica_groups=mesh['req'=8,'cfg'=2,'seq'=2] {'seq'}, dimensions={1} | all-to-all | bytes 1048576 | tf_op jit(solution)/shard_map/all_to_all | solution.py:121
  37.7 3.5 %all-to-all-start.1 = ((bf16[256,2,512]{2,0,1:T(8,128)(2,1)}), bf16[256,2,512]{2,0,1:T(8,128)(2,1)S(1)}, u32[]{:S(2)}, u32[]{:S(2)}) async-start(bf16[256,2,512]{2,0,1:T(8,128)(2,1)} %get-tuple-element.33), calls=%async_computation.1 | async-start | bytes 1048576 | tf_op jit(solution)/shard_map/all_to_all | solution.py:122
  41.2 0.4 all_to_all.50
  41.5 0.9 copy.24
  42.4 5.0 %all-to-all-done.1 = bf16[256,2,512]{2,0,1:T(8,128)(2,1)S(1)} async-done(((bf16[256,2,512]{2,0,1:T(8,128)(2,1)}), bf16[256,2,512]{2,0,1:T(8,128)(2,1)S(1)}, u32[]{:S(2)}, u32[]{:S(2)}) %all-to-all-start.1) | async-done | bytes 524320 | tf_op jit(solution)/shard_map/all_to_all | solution.py:122
  47.4 3.5 %all-to-all-start.2 = ((bf16[256,2,512]{2,0,1:T(8,128)(2,1)}), bf16[256,2,512]{2,0,1:T(8,128)(2,1)S(1)}, u32[]{:S(2)}, u32[]{:S(2)}) async-start(bf16[256,2,512]{2,0,1:T(8,128)(2,1)} %copy.24), calls=%async_computation.2 | async-start | bytes 1048576 | tf_op jit(solution)/shard_map/all_to_all | solution.py:123
  53.1 3.6 %all-to-all-done.2 = bf16[256,2,512]{2,0,1:T(8,128)(2,1)S(1)} async-done(((bf16[256,2,512]{2,0,1:T(8,128)(2,1)}), bf16[256,2,512]{2,0,1:T(8,128)(2,1)S(1)}, u32[]{:S(2)}, u32[]{:S(2)}) %all-to-all-start.2) | async-done | bytes 524320 | tf_op jit(solution)/shard_map/all_to_all | solution.py:123
  56.8 0.7 fusion.20
  57.5 1.4 %fusion.35 = (f32[4,512]{1,0:T(4,128)S(1)}, f32[4,512,512]{1,2,0:T(8,128)S(1)}) fusion(f32[4,512,512]{1,2,0:T(8,128)S(1)} %fusion.20, pred[512]{0:T(512)(128)(4,1)S(1)} %iota_compare_fusion), kind=kOutput, calls=%fused_computation.79 | output fusion | flops 6291967 | bytes 8397312 | tf_op jit(solution)/shard_map/while/body/eval_jaxpr/sub | solution.py:87
  59.0 0.9 %fusion.8 = bf16[512,4,128]{2,0,1:T(8,128)(2,1)S(1)} fusion(f32[4,512,512]{1,2,0:T(8,128)S(1)} %get-tuple-element.38, f32[4,512]{1,0:T(4,128)S(1)} %get-tuple-element.37, bf16[512,4,128]{2,1,0:T(4,128)(2,1)S(1)} %reshape.283), kind=kOutput, calls=%fused_computation.14 | convolution fusion | flops 270794752 | bytes 5251072 | tf_op jit(solution)/shard_map/while/body/eval_jaxpr/hqk,khd->qhd/dot_general | solution.py:90
  59.9 0.4 copy.27
  60.3 1.0 %all_to_all.53 = bf16[2,256,512]{2,1,0:T(8,128)(2,1)} reshape(bf16[512,4,128]{2,1,0:T(4,128)(2,1)S(1)} %copy.27) | data formatting | bytes 1048576 | tf_op jit(solution)/shard_map/all_to_all | solution.py:132
  61.3 3.5 %all-to-all-start.3 = ((bf16[2,256,512]{2,1,0:T(8,128)(2,1)}), bf16[2,256,512]{2,1,0:T(8,128)(2,1)S(1)}, u32[]{:S(2)}, u32[]{:S(2)}) async-start(bf16[2,256,512]{2,1,0:T(8,128)(2,1)} %all_to_all.53), calls=%async_computation.3 | async-start | bytes 1048576 | tf_op jit(solution)/shard_map/all_to_all | solution.py:132
  64.9 5.7 %all-to-all-done.3 = bf16[2,256,512]{2,1,0:T(8,128)(2,1)S(1)} async-done(((bf16[2,256,512]{2,1,0:T(8,128)(2,1)}), bf16[2,256,512]{2,1,0:T(8,128)(2,1)S(1)}, u32[]{:S(2)}, u32[]{:S(2)}) %all-to-all-start.3) | async-done | bytes 524320 | tf_op jit(solution)/shard_map/all_to_all | solution.py:132
  70.7 0.2 copy.28
  70.9 1.1 %all-gather.2.cloned.1.call-done = bf16[1024,1536]{1,0:T(8,128)(2,1)} async-done(((bf16[128,1536]{1,0:T(8,128)(2,1)}), bf16[1024,1536]{1,0:T(8,128)(2,1)}) %all-gather.2.cloned.1.call-update) | async-done | bytes 3145744 | tf_op jit(solution)/shard_map/all_gather | solution.py:135
  71.9 3.0 %fusion.36 = (f32[256]{0:T(256)S(1)}, f32[256,1536]{1,0:T(8,128)S(1)}) fusion(bf16[256,1024]{0,1:T(8,128)(2,1)S(1)} %bitcast.69, bf16[1024,1536]{1,0:T(8,128)(2,1)} %all-gather.2.cloned.1.call-done, f32[1536]{0:T(1024)S(1)} %reduce, bf16[1,1,256,1536]{3,2,1,0:T(8,128)(2,1)S(1)} %copy-done.7), kind=kOutput, calls=%fused_computation.80 | convolution fusion | flops 806878976 | bytes 6036480 | tf_op jit(solution)/shard_map/dot_general | solution.py:133
  74.9 0.3 multiply_reduce_fusion
  75.3 0.5 convolution_add_fusion
  75.8 3.2 %collective-permute-start = (f32[256,32]{0,1:T(8,128)S(1)}, f32[256,32]{0,1:T(8,128)S(1)}, u32[]{:S(2)}, u32[]{:S(2)}) collective-permute-start(f32[256,32]{0,1:T(8,128)S(1)} %constant_dynamic-slice_fusion), channel_id=1, source_target_pairs={{0,2},{2,0},{1,3},{3,1},{4,6},{6,4},{5,7},{7,5},{8,10},{10,8},{9,1... | collective-permute-start | bytes 98312 | tf_op jit(solution)/shard_map/ppermute | solution.py:21
  80.4 0.6 fusion.25
  (37 shorter events, 1.2 us)
Async XLA Ops:
  7.2 68.1 %copy-start = (bf16[1536,64]{0,1:T(8,128)(2,1)S(1)}, bf16[1536,64]{0,1:T(8,128)(2,1)}, u32[]{:S(2)}) copy-start(bf16[1536,64]{0,1:T(8,128)(2,1)} %param.18) | copy-start | bytes 589828
  7.2 12.1 %copy-start.1 = (bf16[1,1,256,1024]{3,2,1,0:T(8,128)(2,1)S(1)}, bf16[1,1,256,1024]{3,2,1,0:T(8,128)(2,1)}, u32[]{:S(2)}) copy-start(bf16[1,1,256,1024]{3,2,1,0:T(8,128)(2,1)} %param.14) | copy-start | bytes 1572868
  7.2 64.7 %all-gather.2.cloned.1.call-start = ((), (), s32[]{:S(2)}) async-start(), calls=%async_computation.4 | async-start | bytes 3538944 | tf_op jit(solution)/shard_map/all_gather | solution.py:135
  19.9 1.1 %copy-start.2 = (bf16[1,1,256,1024]{3,2,1,0:T(8,128)(2,1)S(1)}, bf16[1,1,256,1024]{3,2,1,0:T(8,128)(2,1)}, u32[]{:S(2)}) copy-start(bf16[1,1,256,1024]{3,2,1,0:T(8,128)(2,1)} %param.13) | copy-start | bytes 1572868
  22.0 19.1 %copy-start.3 = (bf16[1,1,256,1024]{3,2,1,0:T(8,128)(2,1)S(1)}, bf16[1,1,256,1024]{3,2,1,0:T(8,128)(2,1)}, u32[]{:S(2)}) copy-start(bf16[1,1,256,1024]{3,2,1,0:T(8,128)(2,1)} %param.15) | copy-start | bytes 1572868
  37.7 9.7 %all-to-all-start.1 = ((bf16[256,2,512]{2,0,1:T(8,128)(2,1)}), bf16[256,2,512]{2,0,1:T(8,128)(2,1)S(1)}, u32[]{:S(2)}, u32[]{:S(2)}) async-start(bf16[256,2,512]{2,0,1:T(8,128)(2,1)} %get-tuple-element.33), calls=%async_computation.1 | async-start | bytes 1048576 | tf_op jit(solution)/shard_map/all_to_all | solution.py:122
  47.4 9.3 %all-to-all-start.2 = ((bf16[256,2,512]{2,0,1:T(8,128)(2,1)}), bf16[256,2,512]{2,0,1:T(8,128)(2,1)S(1)}, u32[]{:S(2)}, u32[]{:S(2)}) async-start(bf16[256,2,512]{2,0,1:T(8,128)(2,1)} %copy.24), calls=%async_computation.2 | async-start | bytes 1048576 | tf_op jit(solution)/shard_map/all_to_all | solution.py:123
  59.9 5.0 %copy-start.6 = (f32[1,1536]{1,0:T(1,128)S(1)}, f32[1,1536]{1,0:T(1,128)}, u32[]{:S(2)}) copy-start(f32[1,1536]{1,0:T(1,128)} %param.20) | copy-start | bytes 18436
  59.9 5.0 %copy-start.5 = (f32[1,2,1536]{2,1,0:T(2,128)S(1)}, f32[1,2,1536]{2,1,0:T(2,128)}, u32[]{:S(2)}) copy-start(f32[1,2,1536]{2,1,0:T(2,128)} %param.21) | copy-start | bytes 36868
  59.9 12.0 %copy-start.7 = (bf16[1,1,256,1536]{3,2,1,0:T(8,128)(2,1)S(1)}, bf16[1,1,256,1536]{3,2,1,0:T(8,128)(2,1)}, u32[]{:S(2)}) copy-start(bf16[1,1,256,1536]{3,2,1,0:T(8,128)(2,1)} %param.16) | copy-start | bytes 2359300
  61.3 9.3 %all-to-all-start.3 = ((bf16[2,256,512]{2,1,0:T(8,128)(2,1)}), bf16[2,256,512]{2,1,0:T(8,128)(2,1)S(1)}, u32[]{:S(2)}, u32[]{:S(2)}) async-start(bf16[2,256,512]{2,1,0:T(8,128)(2,1)} %all_to_all.53), calls=%async_computation.3 | async-start | bytes 1048576 | tf_op jit(solution)/shard_map/all_to_all | solution.py:132
  71.9 3.3 %copy-start.8 = (f32[64]{0:T(128)S(1)}, f32[64]{0:T(128)}, u32[]{:S(2)}) copy-start(f32[64]{0:T(128)} %param.19) | copy-start | bytes 772
  74.9 5.5 %copy-start.4 = (f32[1,256,32]{1,2,0:T(8,128)S(1)}, f32[1,256,32]{1,2,0:T(8,128)}, u32[]{:S(2)}) copy-start(f32[1,256,32]{1,2,0:T(8,128)} %param.25) | copy-start | bytes 98308
  75.8 4.6 %collective-permute-start = (f32[256,32]{0,1:T(8,128)S(1)}, f32[256,32]{0,1:T(8,128)S(1)}, u32[]{:S(2)}, u32[]{:S(2)}) collective-permute-start(f32[256,32]{0,1:T(8,128)S(1)} %constant_dynamic-slice_fusion), channel_id=1, source_target_pairs={{0,2},{2,0},{1,3},{3,1},{4,6},{6,4},{5,7},{7,5},{8,10},{10,8},{9,1... | collective-permute-start | bytes 98312 | tf_op jit(solution)/shard_map/ppermute | solution.py:21
Sparse Core Ops, SparseCore 0:
  10.2 61.6 all-gather.1
where the time goes:
time: 88.6 us; the launch traced here: 87.9 us
  between operations  22.4 us (25%)
  waiting for transfers between devices  16 us (18%)
  starting transfers between devices  13.7 us (15%)
  local copies, waits for them, and re-layouts  10.5 us (12%)
  blocking collectives  10.2 us (12%)
  other arithmetic  10.1 us (11%)
  matrix products  5.09 us (6%)
    all_to_all x1, blocking collectives, on_device(): lax.all_to_all(rot_q, 'seq', split_axis=1, concat_axis=0, tiled=True)  10.2 us
    all_to_all x1, waiting for transfers between devices, on_device(): lax.all_to_all(head_result, 'seq', split_axis=0, concat_axis=1, tiled=True)  5.72 us
    convert_element_type x1, other arithmetic, rotary(): return turned.astype(jnp.bfloat16)  5.45 us
    all_to_all x1, waiting for transfers between devices, on_device(): lax.all_to_all(rot_k, 'seq', split_axis=1, concat_axis=0, tiled=True)  4.96 us
    convert_element_type x2, local copies, waits for them, and re-layouts, rotary(): source = vectors.astype(jnp.float32)  4.14 us
    all_to_all x1, waiting for transfers between devices, on_device(): lax.all_to_all(values[0, 0], 'seq', split_axis=1, concat_axis=0, tiled=True)  3.57 us
    all_to_all x1, starting transfers between devices, on_device(): lax.all_to_all(rot_k, 'seq', split_axis=1, concat_axis=0, tiled=True)  3.49 us
    all_to_all x1, starting transfers between devices, on_device(): lax.all_to_all(values[0, 0], 'seq', split_axis=1, concat_axis=0, tiled=True)  3.49 us
  transfers between devices with their start and end apart: 5, of which 4 were waited for; matrix products, arithmetic and copies ran while one was open for 22% of the time, Pallas kernels for 0%

commit v1 on v0

--- a/solution.py
+++ b/solution.py
@@ -118,7 +118,10 @@
     rot_q = rotary(queries[0, 0], grid_dims, first_token)
     rot_k = rotary(key_vectors[0, 0], grid_dims, first_token)
     head_q, head_k, head_v = (
-        lax.all_to_all(rot_q, "seq", split_axis=1, concat_axis=0, tiled=True),
+        jnp.concatenate(
+            lax.all_to_all(jnp.stack(jnp.split(rot_q, lax.axis_size("seq"), axis=1)), "seq", 0, 0),
+            axis=0,
+        ),
         lax.all_to_all(rot_k, "seq", split_axis=1, concat_axis=0, tiled=True),
         lax.all_to_all(values[0, 0], "seq", split_axis=1, concat_axis=0, tiled=True),
     )

time: 88.6 us -> 92.8 us (1.047)
  blocking collectives: 10.2 us -> 0 us
  other arithmetic: 10.1 us -> 17.4 us
  starting transfers between devices: 13.7 us -> 16.9 us
  waiting for transfers between devices: 16 us -> 18.2 us
  local copies, waits for them, and re-layouts: 10.5 us -> 12.2 us
    all_to_all x1 -> x0, blocking collectives: 10.2 us -> none  [on_device(): lax.all_to_all(rot_q, 'seq', split_axis=1, concat_axis=0, tiled=True)]
    convert_element_type x1 -> x2, other arithmetic: 5.45 us -> 11.2 us  [rotary(): return turned.astype(jnp.bfloat16)]
    all_to_all x1, waiting for transfers between devices: 4.96 us -> 0.01 us  [on_device(): lax.all_to_all(rot_k, 'seq', split_axis=1, concat_axis=0, tiled=True)]
    all_to_all x0 -> x1, waiting for transfers between devices: none -> 4.83 us  [on_device(): lax.all_to_all(jnp.stack(jnp.split(rot_q, lax.axis_size('seq'), axis=1)),...]
    all_to_all x0 -> x1, starting transfers between devices: none -> 3.49 us  [on_device(): lax.all_to_all(jnp.stack(jnp.split(rot_q, lax.axis_size('seq'), axis=1)),...]
    all_to_all x1, waiting for transfers between devices: 3.57 us -> 6.6 us  [on_device(): lax.all_to_all(values[0, 0], 'seq', split_axis=1, concat_axis=0, tiled=True)]
    all_to_all x2, local copies, waits for them, and re-layouts: 1.24 us -> 4.11 us  [on_device(): lax.all_to_all(values[0, 0], 'seq', split_axis=1, concat_axis=0, tiled=True)]
    convert_element_type x2 -> x1, local copies, waits for them, and re-layouts: 4.14 us -> 2.07 us  [rotary(): source = vectors.astype(jnp.float32)]
  transfers between devices with their start and end apart: 5 -> 6, of which waited for: 4 -> 3; matrix products, arithmetic and copies ran while one was open for 22% -> 29% of each run, Pallas kernels for 0% -> 0%
where the time goes in v1:
time: 92.8 us; the launch traced here: 91.9 us
  between operations  22.2 us (24%)
  waiting for transfers between devices  18.2 us (20%)
  other arithmetic  17.4 us (19%)
  starting transfers between devices  16.9 us (18%)
  local copies, waits for them, and re-layouts  12.2 us (13%)
  matrix products  5.09 us (5%)
    convert_element_type x2, other arithmetic, rotary(): return turned.astype(jnp.bfloat16)  11.2 us
    all_to_all x1, waiting for transfers between devices, on_device(): lax.all_to_all(values[0, 0], 'seq', split_axis=1, concat_axis=0, tiled=True)  6.6 us
    all_to_all x1, waiting for transfers between devices, on_device(): lax.all_to_all(head_result, 'seq', split_axis=0, concat_axis=1, tiled=True)  6.02 us
    all_to_all x1, waiting for transfers between devices, on_device(): lax.all_to_all(jnp.stack(jnp.split(rot_q, lax.axis_size('seq'), axis=1)),...  4.83 us
    all_to_all x2, local copies, waits for them, and re-layouts, on_device(): lax.all_to_all(values[0, 0], 'seq', split_axis=1, concat_axis=0, tiled=True)  4.11 us
    all_to_all x1, starting transfers between devices, on_device(): lax.all_to_all(jnp.stack(jnp.split(rot_q, lax.axis_size('seq'), axis=1)),...  3.49 us
    all_to_all x1, starting transfers between devices, on_device(): lax.all_to_all(values[0, 0], 'seq', split_axis=1, concat_axis=0, tiled=True)  3.49 us
    all_to_all x1, starting transfers between devices, on_device(): lax.all_to_all(rot_k, 'seq', split_axis=1, concat_axis=0, tiled=True)  3.49 us
  transfers between devices with their start and end apart: 6, of which 3 were waited for; matrix products, arithmetic and copies ran while one was open for 29% of the time, Pallas kernels for 0%

profile of v1, /device:TPU:1, one launch (start us, length us, event | category | flops | bytes accessed | tf_op | source)
XLA Modules:
  0.0 91.9 jit_solution(11924851170473194500)
XLA Ops:
  7.2 0.7 all-gather.2.cloned.1.call-update
  7.9 1.4 %fusion.40 = (s32[1,1]{1,0:T(1,128)}, s32[1,1]{1,0:T(1,128)}, s32[1,1]{1,0:T(1,128)}) fusion(s32[1,3]{1,0:T(1,128)} %param.22), kind=kLoop, calls=%fused_computation.94 | loop fusion | bytes 24 | tf_op jit(solution)/shard_map/slice | solution.py:116
  13.9 2.1 %reshape.244 = f32[256,2,512]{2,1,0:T(2,128)S(1)} reshape(bf16[1,1,256,1024]{3,2,1,0:T(8,128)(2,1)} %param.14) | data formatting | bytes 1572864 | tf_op jit(solution)/shard_map/convert_element_type | solution.py:51
  16.0 0.9 and_select_fusion.3
  17.0 1.2 %convert_bitcast_fusion = f32[256,1024]{1,0:T(8,128)S(1)} fusion(bf16[1,1,256,1024]{3,2,1,0:T(8,128)(2,1)} %param.14), kind=kLoop, calls=%fused_computation.38 | loop fusion | flops 262144 | bytes 1572864 | tf_op jit(solution)/shard_map/convert_element_type | solution.py:51
  18.3 0.4 fusion.38
  18.7 0.4 pad_maximum_fusion
  19.1 5.2 %fusion.11 = bf16[256,2,512]{2,0,1:T(8,128)(2,1)} fusion(f32[32,2,8,512]{3,2,1,0:T(8,128)S(1)} %bitcast.54, f32[32,2,8,512]{3,2,1,0:T(8,128)S(1)} %bitcast.53, f32[256,2,512]{2,1,0:T(2,128)S(1)} %reshape.244, f32[2,512]{1,0:T(2,128)S(1)} %get-tuple-element.48, f32[2,512]{1,0:T(2,128)S(1)} %get-tuple-element.47, s32[256]{0:T(256)S(1)} %get-tuple-element.43, ...), kind=kLoop, calls=%fused_computation.19 | loop fusion | flops 2621440 | bytes 3684352 | tf_op jit(solution)/shard_map/convert_element_type | solution.py:55
  24.4 3.5 %all-to-all-start.1 = ((bf16[256,2,512]{2,0,1:T(8,128)(2,1)}), bf16[256,2,512]{2,0,1:T(8,128)(2,1)S(1)}, u32[]{:S(2)}, u32[]{:S(2)}) async-start(bf16[256,2,512]{2,0,1:T(8,128)(2,1)} %fusion.11), calls=%async_computation.1 | async-start | bytes 1048576 | tf_op jit(solution)/shard_map/all_to_all | solution.py:125
  28.0 0.7 fusion.36
  28.7 0.4 fusion.37
  29.2 2.2 %all_to_all.42 = bf16[256,2,512]{2,1,0:T(2,128)(2,1)} reshape(bf16[1,1,256,1024]{3,2,1,0:T(8,128)(2,1)} %param.15) | data formatting | bytes 1048576 | tf_op jit(solution)/shard_map/all_to_all | solution.py:126
  31.4 1.9 %copy.21 = bf16[256,2,512]{2,0,1:T(8,128)(2,1)} copy(bf16[256,2,512]{2,1,0:T(2,128)(2,1)} %all_to_all.42) | data formatting | bytes 1048576 | tf_op jit(solution)/shard_map/all_to_all | solution.py:126
  33.3 6.0 %fusion.14 = bf16[256,1024]{1,0:T(8,128)(2,1)} fusion(f32[256,1]{1,0:T(8,128)} %get-tuple-element.17, f32[256,1023]{1,0:T(8,128)S(1)} %get-tuple-element.25, f32[256,1023]{1,0:T(8,128)S(1)} %get-tuple-element.24, f32[256,1]{1,0:T(8,128)S(1)} %get-tuple-element.16, f32[1024]{0:T(1024)S(1)} %get-tuple-element.52, f32[1024]{0:T(1024)S(1)} %get-tuple-element.51, ...), kind=kLoop, calls=%fused_computation.23 | loop fusion | flops 3407872 | bytes 3160064 | tf_op jit(solution)/shard_map/convert_element_type | solution.py:55
  39.3 3.5 %all-to-all-start.2 = ((bf16[256,2,512]{2,0,1:T(8,128)(2,1)}), bf16[256,2,512]{2,0,1:T(8,128)(2,1)S(1)}, u32[]{:S(2)}, u32[]{:S(2)}) async-start(bf16[256,2,512]{2,0,1:T(8,128)(2,1)} %copy.21), calls=%async_computation.2 | async-start | bytes 1048576 | tf_op jit(solution)/shard_map/all_to_all | solution.py:126
  42.8 1.1 %slice_bitcast_fusion.1 = (bf16[1,256,512]{2,1,0:T(8,128)(2,1)S(1)}, bf16[1,256,512]{2,1,0:T(8,128)(2,1)S(1)}) fusion(bf16[256,1024]{1,0:T(8,128)(2,1)} %fusion.14), kind=kLoop, calls=%fused_computation.37 | loop fusion | bytes 1048576 | tf_op jit(solution)/shard_map/stack | solution.py:122
  43.8 0.9 pad_maximum_fusion.2
  44.7 6.6 %all-to-all-done.2 = bf16[256,2,512]{2,0,1:T(8,128)(2,1)S(1)} async-done(((bf16[256,2,512]{2,0,1:T(8,128)(2,1)}), bf16[256,2,512]{2,0,1:T(8,128)(2,1)S(1)}, u32[]{:S(2)}, u32[]{:S(2)}) %all-to-all-start.2) | async-done | bytes 524320 | tf_op jit(solution)/shard_map/all_to_all | solution.py:126
  51.3 3.5 %all-to-all-start = ((bf16[2,256,512]{2,1,0:T(8,128)(2,1)}), bf16[2,256,512]{2,1,0:T(8,128)(2,1)S(1)}, u32[]{:S(2)}, u32[]{:S(2)}) async-start(bf16[2,256,512]{2,1,0:T(8,128)(2,1)} %pad_maximum_fusion.2), calls=%async_computation | async-start | bytes 1048576 | tf_op jit(solution)/shard_map/all_to_all | solution.py:122
  57.0 4.8 %all-to-all-done = bf16[2,256,512]{2,1,0:T(8,128)(2,1)S(1)} async-done(((bf16[2,256,512]{2,1,0:T(8,128)(2,1)}), bf16[2,256,512]{2,1,0:T(8,128)(2,1)S(1)}, u32[]{:S(2)}, u32[]{:S(2)}) %all-to-all-start) | async-done | bytes 524320 | tf_op jit(solution)/shard_map/all_to_all | solution.py:122
  62.0 0.7 fusion.19
  62.7 1.4 %fusion.41 = (f32[4,512]{1,0:T(4,128)S(1)}, f32[4,512,512]{1,2,0:T(8,128)S(1)}) fusion(f32[4,512,512]{1,2,0:T(8,128)S(1)} %fusion.19, pred[512]{0:T(512)(128)(4,1)S(1)} %iota_compare_fusion), kind=kOutput, calls=%fused_computation.95 | output fusion | flops 6291967 | bytes 8397312 | tf_op jit(solution)/shard_map/while/body/eval_jaxpr/sub | solution.py:87
  64.1 0.9 fusion.8
  65.1 0.4 copy.24
  65.5 1.0 %all_to_all.45 = bf16[2,256,512]{2,1,0:T(8,128)(2,1)} reshape(bf16[512,4,128]{2,1,0:T(4,128)(2,1)S(1)} %copy.24) | data formatting | bytes 1048576 | tf_op jit(solution)/shard_map/all_to_all | solution.py:135
  66.5 3.5 %all-to-all-start.3 = ((bf16[2,256,512]{2,1,0:T(8,128)(2,1)}), bf16[2,256,512]{2,1,0:T(8,128)(2,1)S(1)}, u32[]{:S(2)}, u32[]{:S(2)}) async-start(bf16[2,256,512]{2,1,0:T(8,128)(2,1)} %all_to_all.45), calls=%async_computation.3 | async-start | bytes 1048576 | tf_op jit(solution)/shard_map/all_to_all | solution.py:135
  70.1 6.0 %all-to-all-done.3 = bf16[2,256,512]{2,1,0:T(8,128)(2,1)S(1)} async-done(((bf16[2,256,512]{2,1,0:T(8,128)(2,1)}), bf16[2,256,512]{2,1,0:T(8,128)(2,1)S(1)}, u32[]{:S(2)}, u32[]{:S(2)}) %all-to-all-start.3) | async-done | bytes 524320 | tf_op jit(solution)/shard_map/all_to_all | solution.py:135
  76.3 3.0 %fusion.42 = (f32[256]{0:T(256)S(1)}, f32[256,1536]{1,0:T(8,128)S(1)}) fusion(bf16[256,1024]{0,1:T(8,128)(2,1)S(1)} %bitcast.58, bf16[1024,1536]{1,0:T(8,128)(2,1)} %all-gather.2.cloned.1.call-done, f32[1536]{0:T(1024)S(1)} %reduce, bf16[1,1,256,1536]{3,2,1,0:T(8,128)(2,1)S(1)} %copy-done.5), kind=kOutput, calls=%fused_computation.96 | convolution fusion | flops 806878976 | bytes 6036480 | tf_op jit(solution)/shard_map/dot_general | solution.py:136
  79.3 0.3 multiply_reduce_fusion
  79.7 0.5 convolution_add_fusion
  80.2 2.9 %collective-permute-start = (f32[256,32]{0,1:T(8,128)S(1)}, f32[256,32]{0,1:T(8,128)S(1)}, u32[]{:S(2)}, u32[]{:S(2)}) collective-permute-start(f32[256,32]{0,1:T(8,128)S(1)} %constant_dynamic-slice_fusion), channel_id=1, source_target_pairs={{0,2},{2,0},{1,3},{3,1},{4,6},{6,4},{5,7},{7,5},{8,10},{10,8},{9,1... | collective-permute-start | bytes 98312 | tf_op jit(solution)/shard_map/ppermute | solution.py:21
  84.5 0.6 fusion.31
  (38 shorter events, 1.2 us)
Async XLA Ops:
  7.2 72.5 %copy-start = (bf16[1536,64]{0,1:T(8,128)(2,1)S(1)}, bf16[1536,64]{0,1:T(8,128)(2,1)}, u32[]{:S(2)}) copy-start(bf16[1536,64]{0,1:T(8,128)(2,1)} %param.18) | copy-start | bytes 589828
  7.2 69.1 %all-gather.2.cloned.1.call-start = ((), (), s32[]{:S(2)}) async-start(), calls=%async_computation.4 | async-start | bytes 3538944 | tf_op jit(solution)/shard_map/all_gather | solution.py:138
  19.1 8.8 %copy-start.1 = (bf16[1,1,256,1024]{3,2,1,0:T(8,128)(2,1)S(1)}, bf16[1,1,256,1024]{3,2,1,0:T(8,128)(2,1)}, u32[]{:S(2)}) copy-start(bf16[1,1,256,1024]{3,2,1,0:T(8,128)(2,1)} %param.13) | copy-start | bytes 1572868
  24.4 14.9 %all-to-all-start.1 = ((bf16[256,2,512]{2,0,1:T(8,128)(2,1)}), bf16[256,2,512]{2,0,1:T(8,128)(2,1)S(1)}, u32[]{:S(2)}, u32[]{:S(2)}) async-start(bf16[256,2,512]{2,0,1:T(8,128)(2,1)} %fusion.11), calls=%async_computation.1 | async-start | bytes 1048576 | tf_op jit(solution)/shard_map/all_to_all | solution.py:125
  39.3 12.0 %all-to-all-start.2 = ((bf16[256,2,512]{2,0,1:T(8,128)(2,1)}), bf16[256,2,512]{2,0,1:T(8,128)(2,1)S(1)}, u32[]{:S(2)}, u32[]{:S(2)}) async-start(bf16[256,2,512]{2,0,1:T(8,128)(2,1)} %copy.21), calls=%async_computation.2 | async-start | bytes 1048576 | tf_op jit(solution)/shard_map/all_to_all | solution.py:126
  51.3 10.5 %all-to-all-start = ((bf16[2,256,512]{2,1,0:T(8,128)(2,1)}), bf16[2,256,512]{2,1,0:T(8,128)(2,1)S(1)}, u32[]{:S(2)}, u32[]{:S(2)}) async-start(bf16[2,256,512]{2,1,0:T(8,128)(2,1)} %pad_maximum_fusion.2), calls=%async_computation | async-start | bytes 1048576 | tf_op jit(solution)/shard_map/all_to_all | solution.py:122
  65.0 5.0 %copy-start.4 = (f32[1,1536]{1,0:T(1,128)S(1)}, f32[1,1536]{1,0:T(1,128)}, u32[]{:S(2)}) copy-start(f32[1,1536]{1,0:T(1,128)} %param.20) | copy-start | bytes 18436
  65.0 5.0 %copy-start.3 = (f32[1,2,1536]{2,1,0:T(2,128)S(1)}, f32[1,2,1536]{2,1,0:T(2,128)}, u32[]{:S(2)}) copy-start(f32[1,2,1536]{2,1,0:T(2,128)} %param.21) | copy-start | bytes 36868
  65.0 11.3 %copy-start.5 = (bf16[1,1,256,1536]{3,2,1,0:T(8,128)(2,1)S(1)}, bf16[1,1,256,1536]{3,2,1,0:T(8,128)(2,1)}, u32[]{:S(2)}) copy-start(bf16[1,1,256,1536]{3,2,1,0:T(8,128)(2,1)} %param.16) | copy-start | bytes 2359300
  66.5 9.6 %all-to-all-start.3 = ((bf16[2,256,512]{2,1,0:T(8,128)(2,1)}), bf16[2,256,512]{2,1,0:T(8,128)(2,1)S(1)}, u32[]{:S(2)}, u32[]{:S(2)}) async-start(bf16[2,256,512]{2,1,0:T(8,128)(2,1)} %all_to_all.45), calls=%async_computation.3 | async-start | bytes 1048576 | tf_op jit(solution)/shard_map/all_to_all | solution.py:135
  76.3 3.3 %copy-start.6 = (f32[64]{0:T(128)S(1)}, f32[64]{0:T(128)}, u32[]{:S(2)}) copy-start(f32[64]{0:T(128)} %param.19) | copy-start | bytes 772
  79.3 5.1 %copy-start.2 = (f32[1,256,32]{1,2,0:T(8,128)S(1)}, f32[1,256,32]{1,2,0:T(8,128)}, u32[]{:S(2)}) copy-start(f32[1,256,32]{1,2,0:T(8,128)} %param.25) | copy-start | bytes 98308
  80.2 4.3 %collective-permute-start = (f32[256,32]{0,1:T(8,128)S(1)}, f32[256,32]{0,1:T(8,128)S(1)}, u32[]{:S(2)}, u32[]{:S(2)}) collective-permute-start(f32[256,32]{0,1:T(8,128)S(1)} %constant_dynamic-slice_fusion), channel_id=1, source_target_pairs={{0,2},{2,0},{1,3},{3,1},{4,6},{6,4},{5,7},{7,5},{8,10},{10,8},{9,1... | collective-permute-start | bytes 98312 | tf_op jit(solution)/shard_map/ppermute | solution.py:21
Sparse Core Ops, SparseCore 0:
  10.2 61.6 all-gather.1
